TPU v7x, 32 devices: a whole 2x2x4 slice. The times are simulated.
32 devices in a mesh: dp: 8 (over y, x, core), mp: 4 (over z).
Axes of the slice: x: 2, y: 2, z: 4, core: 2. Of those that a mesh axis runs over, the one named last changes fastest.
Arguments:
- hidden: bfloat16 [32, 512, 1024], P(('dp', 'mp')), may hold values from -90 to 90
- positions: int32 [32, 80], P(('dp', 'mp')), may hold values from 0 to 511, as said below
- targets: int32 [32, 80], P(('dp', 'mp')), may hold values from 0 to 32767
- counts: int32 [32], P(('dp', 'mp')), may hold values from 1 to 80, 1920 in all
- dense_weight: bfloat16 [1024, 1024], replicated, may hold values from -1 to 1
- dense_bias: float32 [1024], replicated, may hold values from -3 to 3
- norm_gain: float32 [1024], replicated, may hold values from 0.4 to 1.6
- norm_shift: float32 [1024], replicated, may hold values from -3 to 3
- embedding: bfloat16 [32768, 1024], P('mp', 'dp'), may hold values from -2 to 2
- vocab_bias: float32 [32768], P('mp'), may hold values from -5 to 5
Outputs:
- loss: float32 [], replicated
- embedding_grad: float32 [32768, 1024], P('mp', 'dp')
Inputs may be any that keep to these rules, and one draw needn't show every extreme that they name: The 80 positions of a sequence are distinct; only the first counts[s] of them are masked. `counts`: some sequence has exactly 80.
All inputs are finite; a program needn't handle non-finite values. No bound on the sum of `counts` on one device may be relied on, other than what follows from the above.
Results may differ from a plain program's by a relative error of at most 0.00041.
Values may be sent and summed in bfloat16 or wider, within the bound.
No kernel may reach another device: no remote copies, remote signals or barrier semaphores. Data moves between devices by JAX's collectives and lax.ppermute only.
A program may use at most 128 MiB of HBM per device.

v0:
```python
import jax
import jax.numpy as jnp
from jax import lax
from jax.sharding import PartitionSpec as P


def merged(part, axis, combine):
    gathered = jax.tree.map(lambda a: lax.all_gather(a, axis), part)

    def take(source):
        return jax.tree.map(lambda a: lax.dynamic_index_in_dim(a, source, 0, False), gathered)

    return lax.fori_loop(
        1, lax.axis_size(axis), lambda source, state: combine(state, take(source)), take(0)
    )


def transform(rows, dense_weight, dense_bias, norm_gain, norm_shift):
    pre = jnp.dot(rows, dense_weight, preferred_element_type=jnp.float32) + dense_bias
    act = jax.nn.gelu(pre, approximate=False)
    mean = jnp.mean(act, axis=-1, keepdims=True)
    centred = act - mean
    var = jnp.mean(centred * centred, axis=-1, keepdims=True)
    return (centred * lax.rsqrt(var + 1e-05) * norm_gain + norm_shift).astype(jnp.bfloat16)


def combine(first, second):
    top = jnp.maximum(first[0], second[0])
    total = first[1] * jnp.exp(first[0] - top) + second[1] * jnp.exp(second[0] - top)
    return (top, total, first[2] + second[2])


def on_device(
    hidden,
    positions,
    targets,
    counts,
    dense_weight,
    dense_bias,
    norm_gain,
    norm_shift,
    embedding,
    vocab_bias,
):
    width = hidden.shape[2]
    slot_count = positions.shape[1]
    own_rows = jnp.take_along_axis(hidden, positions[:, :, None], axis=1).reshape(-1, width)
    gathered = lax.all_gather(own_rows, "mp", axis=0, tiled=True)
    normed = transform(gathered, dense_weight, dense_bias, norm_gain, norm_shift)
    group_targets, group_counts = (
        lax.all_gather(targets, "mp", axis=0, tiled=True),
        lax.all_gather(counts, "mp", axis=0, tiled=True),
    )
    labels = group_targets.reshape(-1)
    slots = jnp.arange(slot_count, dtype=jnp.int32)
    valid = (slots[None, :] < group_counts[:, None]).reshape(-1)
    shard = embedding.shape[0]
    logits = (
        lax.dot_general(
            normed,
            lax.all_gather(embedding, "dp", axis=1, tiled=True),
            (((1,), (1,)), ((), ())),
            preferred_element_type=jnp.float32,
        )
        + vocab_bias
    )
    first_id = lax.axis_index("mp") * shard
    vocab_ids = first_id + jnp.arange(shard, dtype=jnp.int32)
    onehot = vocab_ids[None, :] == labels[:, None]
    local_picked = jnp.sum(jnp.where(onehot, logits, 0.0), axis=1)
    local_top = jnp.max(logits, axis=1)
    local_total = jnp.sum(jnp.exp(logits - local_top[:, None]), axis=1)
    top, total, picked = merged((local_top, local_total, local_picked), "mp", combine)
    lse = top + jnp.log(total)
    group_loss = jnp.sum(jnp.where(valid, lse - picked, 0.0))
    grad_rows = jnp.where(
        valid[:, None], jnp.exp(logits - lse[:, None]) - onehot.astype(jnp.float32), 0.0
    ).astype(jnp.bfloat16)
    group_total = jnp.sum(group_counts.astype(jnp.float32))
    loss_sum, mask_total = lax.psum((group_loss, group_total), "dp")
    partial_grad = lax.dot_general(
        grad_rows, normed, (((0,), (0,)), ((), ())), preferred_element_type=jnp.float32
    )
    embedding_grad = lax.psum_scatter(partial_grad, "dp", scatter_dimension=1, tiled=True)
    return (loss_sum / mask_total, embedding_grad)


def solution(mesh):
    in_specs = (
        P(("dp", "mp"), None, None),
        P(("dp", "mp"), None),
        P(("dp", "mp"), None),
        P(("dp", "mp")),
        P(),
        P(),
        P(),
        P(),
        P("mp", "dp"),
        P("mp"),
    )
    out_specs = (P(), P("mp", "dp"))
    return jax.shard_map(
        on_device, mesh=mesh, in_specs=in_specs, out_specs=out_specs, check_vma=False
    )
```

profile of v0, /device:TPU:0, one launch (start us, length us, event | category | flops | bytes accessed | tf_op | source)
XLA Modules:
  0.0 377.4 jit_solution(1105444352639941221)
XLA Ops:
  7.2 0.0 copy-start
  7.2 0.0 copy-start.9
  7.2 0.0 copy-start.5
  7.2 0.0 copy-start.8
  7.2 0.0 copy-start.2
  7.2 0.0 all-gather.6.cloned.1.call-start
  7.3 0.7 all-gather.6.cloned.1.call-update
  8.0 0.0 reduce-scatter.2.cloned.1.call-start
  8.7 0.0 copy-done.9
  8.7 0.6 dynamic-slice
  9.3 0.8 dynamic-update-slice
  10.0 9.9 %all-reduce = s32[4]{0:T(128)S(1)} all-reduce(s32[4]{0:T(128)S(1)} %dynamic-update-slice), channel_id=1, replica_groups=mesh['dp'=8,'mp'=4] {'mp'}, use_global_device_ids=true, to_apply=%add | all-reduce | flops 4 | bytes 32
  20.6 0.1 iota_compare_fusion
  20.7 0.1 lt.74
  20.8 0.0 copy-done.5
  20.8 9.1 %all-gather.3 = s32[4,1,80]{2,1,0:T(1,128)S(1)} all-gather(s32[1,1,80]{2,1,0:T(1,128)S(1)} %bitcast.14), channel_id=1, replica_groups=mesh['dp'=8,'mp'=4] {'mp'}, dimensions={0}, use_global_device_ids=true | all-gather | bytes 1600 | tf_op jit(solution)/shard_map/all_gather | solution.py:51
  29.9 0.5 broadcast.102
  30.4 0.6 reduce.9
  31.0 0.1 eq.16
  31.1 0.0 copy-done.8
  31.1 0.0 copy-done.2
  31.1 0.0 copy-start.7
  31.1 0.7 gather_fusion
  31.9 0.1 broadcast_select_fusion
  32.0 15.8 %all_gather.31 = bf16[320,1024]{1,0:T(8,128)(2,1)S(1)} all-gather(bf16[80,1024]{1,0:T(8,128)(2,1)S(1)} %broadcast_select_fusion), channel_id=1, replica_groups=mesh['dp'=8,'mp'=4] {'mp'}, dimensions={0}, use_global_device_ids=true | all-gather | bytes 819200 | tf_op jit(solution)/shard_map/all_gather | solution.py:48
  47.8 0.0 copy-done
  47.8 0.0 copy-done.7
  47.8 8.2 %fusion.22 = (f32[320]{0:T(512)S(1)}, f32[320,1024]{1,0:T(8,128)S(1)}) fusion(f32[1024]{0:T(1024)S(1)} %copy-done.7, bf16[320,1024]{1,0:T(8,128)(2,1)S(1)} %all_gather.31, bf16[1024,1024]{1,0:T(8,128)(2,1)S(1)} %copy-done), kind=kOutput, calls=%fused_computation.54 | convolution fusion | flops 692715200 | bytes 4068608 | tf_op jit(solution)/shard_map/dot_general | solution.py:19
  56.0 0.0 copy-start.3
  56.0 0.0 copy-start.4
  56.0 0.0 copy-start.6
  56.0 0.3 multiply_reduce_fusion
  56.3 49.4 %all-gather.6.cloned.1.call-done = bf16[8192,1024]{1,0:T(8,128)(2,1)} async-done(((bf16[8192,128]{1,0:T(8,128)(2,1)}), bf16[8192,1024]{1,0:T(8,128)(2,1)}) %all-gather.6.cloned.1.call-update) | async-done | bytes 16777232 | tf_op jit(solution)/shard_map/all_gather | solution.py:61
  105.7 0.0 copy-done.3
  105.7 0.0 copy-done.4
  105.7 0.0 copy-done.6
  105.7 11.8 %fusion.23 = (f32[320]{0:T(512)S(1)}, f32[320,8192]{1,0:T(8,128)}) fusion(f32[8192]{0:T(1024)S(1)} %copy-done.6, bf16[8192,1024]{1,0:T(8,128)(2,1)} %all-gather.6.cloned.1.call-done, f32[320,1024]{1,0:T(8,128)S(1)} %get-tuple-element.211, f32[1024]{0:T(1024)S(1)} %copy-done.3, f32[1024]{0:T(1024)S(1)} %copy-done.4, f32[320]{0:T(512)S(1)} %add_rsqrt_fusion, ...), kind=kOutput, calls=%fused_computation.55 | convolution fusion | flops 5375589888 | bytes 28618496 | tf_op jit(solution)/shard_map/dot_general | solution.py:59
  117.5 0.2 dynamic-update-slice.1
  117.7 6.8 %fusion = (f32[320]{0:T(512)S(1)}, f32[320]{0:T(512)S(1)}) fusion(f32[320,8192]{1,0:T(8,128)} %get-tuple-element.213, s32[8192]{0:T(1024)S(1)} %iota_add_fusion, s32[320]{0:T(512)S(1)} %eq.16, f32[320]{0:T(512)S(1)} %get-tuple-element.212), kind=kLoop, calls=%fused_computation.8 | loop fusion | flops 13106560 | bytes 10523648 | tf_op jit(solution)/shard_map/reduce_sum | solution.py:70
  124.5 0.3 dynamic-update-slice.3
  124.8 0.3 dynamic-update-slice.2
  125.1 19.0 %all-reduce.5 = (f32[1280]{0:T(1024)S(1)}, f32[1280]{0:T(1024)S(1)}, f32[1280]{0:T(1024)S(1)}) all-reduce(f32[1280]{0:T(1024)S(1)} %dynamic-update-slice.1, f32[1280]{0:T(1024)S(1)} %dynamic-update-slice.2, f32[1280]{0:T(1024)S(1)} %dynamic-update-slice.3), channel_id=2, replica_groups=mesh['dp'=8,'mp'=4] {'mp'}, use_global_device_ids=true, to_apply=%add.1 | all-reduce | flops 3840 | bytes 30720
  144.0 0.1 reshape.129
  144.1 0.1 reshape.130
  144.2 0.1 reshape.131
  144.3 0.3 while.19
  144.6 0.6 select_reduce_fusion
  145.2 21.5 %fusion.4 = f32[8192,1024]{1,0:T(8,128)} fusion(f32[320,8192]{1,0:T(8,128)} %get-tuple-element.213, f32[320]{0:T(512)S(1)} %get-tuple-element.207, s32[8192]{0:T(1024)S(1)} %iota_add_fusion, s32[320]{0:T(512)S(1)} %eq.16, pred[320]{0:T(512)(128)(4,1)S(1)} %lt.74, f32[320,1024]{1,0:T(8,128)S(1)} %get-tuple-element.211, f32[1024]{0:T(1024)S(1)} %copy-done.3, ...), kind=kOutput, calls=%fused_computation.13 | convolution fusion | flops 5386076160 | bytes 45397312 | tf_op jit(solution)/shard_map/dot_general | solution.py:81
  166.7 0.0 reduce-scatter.2.cloned.1.call-update
  166.7 0.0 copy-start.1
  166.7 0.7 convert_reduce_fusion
  167.4 12.5 %all-reduce.4 = (f32[]{:T(128)}, f32[]{:T(128)}) all-reduce(f32[]{:T(128)} %get-tuple-element.206, f32[]{:T(128)} %convert_reduce_fusion), channel_id=1, replica_groups=mesh['dp'=8,'mp'=4] {'dp'}, use_global_device_ids=true, to_apply=%region_8.9 | all-reduce | flops 2 | bytes 16 | tf_op jit(solution)/shard_map/psum | solution.py:80
  181.3 188.1 %reduce-scatter.2.cloned.1.call-done = f32[8192,128]{1,0:T(8,128)} async-done(((f32[8192,1024]{1,0:T(8,128)}), f32[8192,128]{1,0:T(8,128)}) %reduce-scatter.2.cloned.1.call-update) | async-done | bytes 4194320 | tf_op jit(solution)/shard_map/reduce_scatter | solution.py:84
  369.4 0.0 copy-done.1
  (25 shorter events, 0.3 us)
Async XLA Ops:
  7.2 40.6 %copy-start = (bf16[1024,1024]{1,0:T(8,128)(2,1)S(1)}, bf16[1024,1024]{1,0:T(8,128)(2,1)}, u32[]{:S(2)}) copy-start(bf16[1024,1024]{1,0:T(8,128)(2,1)} %param.16) | copy-start | bytes 6291460
  7.2 1.5 copy-start.9
  7.2 13.6 %copy-start.5 = (s32[1,80]{1,0:T(1,128)S(1)}, s32[1,80]{1,0:T(1,128)}, u32[]{:S(2)}) copy-start(s32[1,80]{1,0:T(1,128)} %param.14) | copy-start | bytes 964
  7.2 23.9 %copy-start.8 = (s32[1,80]{1,0:T(1,128)S(1)}, s32[1,80]{1,0:T(1,128)}, u32[]{:S(2)}) copy-start(s32[1,80]{1,0:T(1,128)} %param.13) | copy-start | bytes 964
  7.2 23.9 %copy-start.2 = (bf16[1,512,1024]{2,1,0:T(8,128)(2,1)S(1)}, bf16[1,512,1024]{2,1,0:T(8,128)(2,1)}, u32[]{:S(2)}) copy-start(bf16[1,512,1024]{2,1,0:T(8,128)(2,1)} %param.12) | copy-start | bytes 3145732
  7.2 98.5 %all-gather.6.cloned.1.call-start = ((), (), s32[]{:S(2)}) async-start(), calls=%async_computation.1 | async-start | bytes 18874368 | tf_op jit(solution)/shard_map/all_gather | solution.py:61
  8.0 361.5 %reduce-scatter.2.cloned.1.call-start = ((), (), s32[]{:S(2)}) async-start(), calls=%async_computation.2 | async-start | bytes 37748736 | tf_op jit(solution)/shard_map/reduce_scatter | solution.py:84
  31.1 16.7 %copy-start.7 = (f32[1024]{0:T(1024)S(1)}, f32[1024]{0:T(1024)}, u32[]{:S(2)}) copy-start(f32[1024]{0:T(1024)} %param.17) | copy-start | bytes 12292
  56.0 49.7 %copy-start.3 = (f32[1024]{0:T(1024)S(1)}, f32[1024]{0:T(1024)}, u32[]{:S(2)}) copy-start(f32[1024]{0:T(1024)} %param.19) | copy-start | bytes 12292
  56.0 49.7 %copy-start.4 = (f32[1024]{0:T(1024)S(1)}, f32[1024]{0:T(1024)}, u32[]{:S(2)}) copy-start(f32[1024]{0:T(1024)} %param.18) | copy-start | bytes 12292
  56.0 49.7 %copy-start.6 = (f32[8192]{0:T(1024)S(1)}, f32[8192]{0:T(1024)}, u32[]{:S(2)}) copy-start(f32[8192]{0:T(1024)} %param.21) | copy-start | bytes 98308
  166.7 202.7 %copy-start.1 = (bf16[1024,1024]{1,0:T(8,128)(2,1)S(1)}, bf16[1024,1024]{1,0:T(8,128)(2,1)}, u32[]{:S(2)}) copy-start(bf16[1024,1024]{1,0:T(8,128)(2,1)} %param.16) | copy-start | bytes 6291460
Sparse Core Ops, SparseCore 0:
  9.9 95.7 all-gather.5
  166.8 202.5 reduce-scatter.1
where the time goes:
time: 378 us; the launch traced here: 377 us
  waiting for transfers between devices  238 us (63%)
  blocking collectives  66.3 us (18%)
  matrix products  41.5 us (11%)
  between operations  18 us (5%)
  other arithmetic  9.25 us (2%)
  local copies, waits for them, and re-layouts  3.94 us (1%)
    reduce_scatter x1, waiting for transfers between devices, on_device(): lax.psum_scatter(partial_grad, 'dp', scatter_dimension=1, tiled=True)  188 us
    all_gather x1, waiting for transfers between devices, on_device(): lax.all_gather(embedding, 'dp', axis=1, tiled=True)  49.4 us
    unnamed x2, blocking collectives  28.9 us
    dot_general x1, matrix products, on_device(): lax.dot_general(grad_rows, normed, (((0,), (0,)), ((), ())), preferred_el...  21.5 us
    all_gather x1, blocking collectives, on_device(): gathered = lax.all_gather(own_rows, 'mp', axis=0, tiled=True)  15.8 us
    psum x1, blocking collectives, on_device(): loss_sum, mask_total = lax.psum((group_loss, group_total), 'dp')  12.5 us
    dot_general x1, matrix products, on_device(): lax.dot_general(normed, lax.all_gather(embedding, 'dp', axis=1, tiled=Tru...  11.8 us
    all_gather x1, blocking collectives, on_device(): lax.all_gather(targets, 'mp', axis=0, tiled=True)  9.13 us
  transfers between devices with their start and end apart: 2, of which 2 were waited for; matrix products, arithmetic and copies ran while one was open for 3% of the time, Pallas kernels for 0%

commit v1 on v0

v1 whole, which is shorter than its diff:
```python
import math

import jax
import jax.numpy as jnp
from jax import lax
from jax.experimental import pallas as pl
from jax.experimental.pallas import tpu as pltpu
from jax.sharding import PartitionSpec as P


F32, BF16, F16 = jnp.float32, jnp.bfloat16, jnp.float16
ANY = pl.BlockSpec(memory_space=pl.ANY)
WHOLE = pl.BlockSpec(memory_space=pltpu.VMEM)
SCALAR = pl.BlockSpec(memory_space=pltpu.SMEM)


def swap(x, axis, k):
    n = lax.axis_size(axis)
    return lax.ppermute(x, axis, [(a, a ^ k) for a in range(n)])


def transform(rows, dense_weight, dense_bias, norm_gain, norm_shift):
    pre = jnp.dot(rows, dense_weight, preferred_element_type=F32) + dense_bias
    act = jax.nn.gelu(pre, approximate=False)
    mean = jnp.mean(act, axis=-1, keepdims=True)
    centred = act - mean
    var = jnp.mean(centred * centred, axis=-1, keepdims=True)
    return (centred * lax.rsqrt(var + 1e-05) * norm_gain + norm_shift).astype(BF16)


def place(blocks, index, order):
    out = jnp.zeros((len(blocks),) + blocks[0].shape, blocks[0].dtype)
    for block, k in zip(blocks, order):
        out = lax.dynamic_update_index_in_dim(out, block, index ^ k, 0)
    return out


def cost(flops, *arrays):
    moved = sum(math.prod(x.shape) * x.dtype.itemsize for x in arrays)
    return pl.CostEstimate(flops=flops, transcendentals=0, bytes_accessed=moved)


def group_of(chips):
    return 2 if chips % 2 == 0 else 1


def row_copies(group, close, away, rows, core):
    piece = close[0].shape[0]
    copies = []
    for n in range(len(close)):
        for side in range(2):
            start = 2 * piece * (n % group) + (core ^ side) * piece
            spot = pl.ds(pl.multiple_of(start, piece), piece)
            copies.append(((close if side == 0 else away)[n], rows.at[n // group, spot]))
    return copies


def score_rows(where, tables, near, far, bias, labels, begin, before, chips):
    here = len(near)
    piece, width = near[0].shape
    entries, fw = tables[0].shape[-2:]
    split = len(tables)
    group = group_of(here)
    lanes = 2 * piece
    block = lanes * group
    loads = max(1, 2 * (split - 1))
    chunk = math.gcd(block, max(256, (1 << 18) // entries))
    chunk = chunk if chunk % 128 == 0 else block
    chunks = block // chunk
    last = begin + here == chips
    kept = chips if last else here

    def body(where_ref, *refs):
        tabs, refs = refs[:split], refs[split:]
        close, away = refs[:here], refs[here : 2 * here]
        bias_ref, labels_ref, before_ref, out, lse, tail, rows, joined, buffer, sems, out_sems = refs[2 * here :]
        chip, core = where_ref[0], where_ref[1]
        copies = [(tabs[0], joined)] if split == 1 else []
        for n in range(chips if split > 1 else 0):
            for side in range(2):
                spot = pl.ds(pl.multiple_of((2 * (chip ^ n) + (core ^ side)) * fw, fw), fw)
                copies.append((tabs[n].at[core] if side == 0 else tabs[chips].at[n], joined.at[:, spot]))
        copies += row_copies(group, close, away, rows, core)
        copies = [pltpu.make_async_copy(a, b, sems.at[n]) for n, (a, b) in enumerate(copies)]
        for copy in copies:
            copy.start()
        ids = where_ref[2] + lax.broadcasted_iota(jnp.int32, (entries, chunk), 0)
        found = jnp.zeros((1, chunk), F32)
        if last:
            for n in range(begin):
                lse[chip ^ n] = before_ref[n]
        for copy in copies[:loads]:
            copy.wait()
        writes = []
        for g in range(here // group):
            for copy in copies[loads + 2 * group * g : loads + 2 * group * (g + 1)]:
                copy.wait()
            part = []
            label = jnp.concatenate([labels_ref[chip ^ (begin + group * g + n)] for n in range(group)], axis=1)
            for c in range(chunks):
                spot = pl.ds(c * chunk, chunk)
                scores = (
                    lax.dot_general(
                        joined[...], rows[g, spot], (((1,), (1,)), ((), ())), preferred_element_type=F32
                    )
                    + bias_ref[...]
                )
                buffer[g, :, spot] = scores
                write = pltpu.make_async_copy(
                    buffer.at[g, :, spot], out.at[g, :, spot], out_sems.at[g * chunks + c]
                )
                write.start()
                writes.append(write)
                hit = ids == label[:, c * chunk : (c + 1) * chunk]
                found += jnp.sum(jnp.where(hit, scores, 0.0), axis=0, keepdims=True)
                top = jnp.max(scores, axis=0, keepdims=True)
                part.append(top + jnp.log(jnp.sum(jnp.exp(scores - top), axis=0, keepdims=True)))
            part = jnp.concatenate(part, axis=1)
            for n in range(group):
                spot = group * g + n
                lse[chip ^ (begin + spot) if last else spot] = part[:, n * lanes : (n + 1) * lanes]
        tail[...] = jnp.full((1, 128), jnp.sum(found))
        for write in writes:
            write.wait()

    return pl.pallas_call(
        body,
        in_specs=[SCALAR] + [ANY] * (split + 2 * here) + [WHOLE, WHOLE, WHOLE],
        out_specs=[ANY, WHOLE, WHOLE],
        out_shape=[
            jax.ShapeDtypeStruct((here // group, entries, block), F32),
            jax.ShapeDtypeStruct((kept, 1, lanes), F32),
            jax.ShapeDtypeStruct((1, 128), F32),
        ],
        scratch_shapes=[
            pltpu.VMEM((here // group, block, width), BF16),
            pltpu.VMEM((entries, width), BF16),
            pltpu.VMEM((here // group, entries, block), F32),
            pltpu.SemaphoreType.DMA((loads + 2 * here,)),
            pltpu.SemaphoreType.DMA((here // group * chunks,)),
        ],
        cost_estimate=cost(2 * entries * here * lanes * width, *tables, *near, *far),
        name="scores",
    )(where, *tables, *near, *far, bias, labels, before)


def table_grad(where, scores, lse, labels, near, far, fw):
    chips = len(near)
    _, entries, block = scores[0].shape
    piece, width = near[0].shape
    lanes = 2 * piece
    group = block // lanes
    blocks = chips // group
    aligned = fw % 128 == 0
    outs, span = (2 * chips, fw) if aligned else (1, width)
    held = len(scores)

    def body(where_ref, lse_ref, labels_ref, *refs):
        score_refs, refs = refs[:held], refs[held:]
        close, away, refs = refs[:chips], refs[chips : 2 * chips], refs[2 * chips :]
        out, rows, values, total, sems = refs
        chip, core = where_ref[0], where_ref[1]
        sources = [ref.at[g] for ref in score_refs for g in range(ref.shape[0])]
        moves, copies = row_copies(group, close, away, rows, core), []
        for g in range(blocks):
            copies.append((sources[g], values.at[g]))
            copies += moves[2 * group * g : 2 * group * (g + 1)]
        each = 2 * group + 1
        copies = [pltpu.make_async_copy(a, b, sems.at[n]) for n, (a, b) in enumerate(copies)]
        for copy in copies:
            copy.start()
        ids = where_ref[2] + lax.broadcasted_iota(jnp.int32, (entries, block), 0)
        for g in range(blocks):
            chosen = [chip ^ (group * g + n) for n in range(group)]
            label = jnp.concatenate([labels_ref[n] for n in chosen], axis=1)
            norm = jnp.concatenate([lse_ref[n] for n in chosen], axis=1)
            for copy in copies[each * g : each * (g + 1)]:
                copy.wait()
            value = values[g]
            hit = ids == label
            grad = jnp.where(label >= 0, jnp.exp(value - norm) - jnp.where(hit, 1.0, 0.0), 0.0)
            part = jnp.dot(grad.astype(BF16), rows[g], preferred_element_type=F32)
            for s in range(outs):
                spot = slice(s * span, (s + 1) * span)
                if g == 0:
                    total[s] = part[:, spot]
                else:
                    total[s] += part[:, spot]
        peak = jnp.maximum(jnp.max(jnp.abs(total[...])), 1e-30)
        power = jnp.floor(14.0 - jnp.log2(jnp.full((1, 128), 1.0, F32) * peak))
        factor = jnp.exp2(power)[:, :1]
        for s in range(outs):
            out[s, :entries] = total[s] * factor
            out[s, entries:] = jnp.broadcast_to(power[:, :1], (8, span))

    return pl.pallas_call(
        body,
        in_specs=[SCALAR, WHOLE, WHOLE] + [ANY] * (held + 2 * chips),
        out_specs=WHOLE,
        out_shape=jax.ShapeDtypeStruct((outs, entries + 8, span), F32),
        scratch_shapes=[
            pltpu.VMEM((blocks, block, width), BF16),
            pltpu.VMEM((blocks, entries, block), F32),
            pltpu.VMEM((outs, entries, span), F32),
            pltpu.SemaphoreType.DMA((blocks + 2 * chips,)),
        ],
        cost_estimate=cost(2 * entries * chips * lanes * width, *scores, *near, *far),
        name="table_grad",
    )(where, lse, labels, *scores, *near, *far)


def on_device(
    hidden, positions, targets, counts, dense_weight, dense_bias, norm_gain, norm_shift, embedding, vocab_bias
):
    ndp, nmp = lax.axis_size("dp"), lax.axis_size("mp")
    i, j = lax.axis_index("dp").astype(jnp.int32), lax.axis_index("mp").astype(jnp.int32)
    chip, core, chips = i // 2, i % 2, ndp // 2
    everyone = ("dp", "mp")
    own, slots = positions.shape
    width = hidden.shape[2]
    shard, fw = embedding.shape
    entries = shard // ndp
    local = own * slots
    where = jnp.stack([chip, core, j * shard + i * entries])

    slices = embedding.reshape(chips, 2, entries, fw)
    tables = [lax.dynamic_index_in_dim(slices, chip, 0, False)]
    for n in range(1, chips):
        block = lax.dynamic_index_in_dim(slices, chip ^ n, 0, False)
        tables.append(swap(block, "dp", 2 * n))
    stacked = jnp.stack([lax.dynamic_index_in_dim(x, core ^ 1, 0, False) for x in tables])
    far_tables = swap(stacked, "dp", 1)
    aligned = fw % 128 == 0
    if aligned:
        tables = tables + [far_tables]
    else:
        mine = place([lax.dynamic_index_in_dim(x, core, 0, False) for x in tables], chip, list(range(chips)))
        other = place([far_tables[n] for n in range(chips)], chip, list(range(chips)))
        pair = jnp.stack([jnp.where(core == 0, mine, other), jnp.where(core == 0, other, mine)], 1)
        tables = [pair.reshape(ndp, entries, fw).transpose(1, 0, 2).reshape(entries, width)]
    bias = lax.dynamic_slice_in_dim(vocab_bias, i * entries, entries).reshape(entries, 1)

    own_rows = jnp.take_along_axis(hidden, positions[:, :, None], axis=1).reshape(-1, width)
    normed = transform(own_rows, dense_weight, dense_bias, norm_gain, norm_shift)
    zs = list(range(1, nmp))
    column = [normed]
    for k in zs:
        column.append(swap(normed, "mp", k))
    column = place(column, j, [0] + zs).reshape(nmp * local, width)
    near = [column]
    for n in range(1, chips):
        near.append(swap(column, "dp", 2 * n))
    far = [swap(x, "dp", 1) for x in near]
    half = chips // 2 if chips % 4 == 0 else chips
    slot_ids = jnp.arange(slots, dtype=jnp.int32)
    labels = jnp.where(slot_ids[None, :] < counts[:, None], targets, -1).reshape(1, -1)
    labels = jnp.broadcast_to(labels, (ndp * nmp, local))
    labels = lax.all_to_all(labels, everyone, 0, 0, tiled=True)
    labels = labels.reshape(chips, 1, -1)
    scores, lse, found = [], bias, 0.0
    for begin in range(0, chips, half):
        part, lse, tail = score_rows(
            where, tables, near[begin : begin + half], far[begin : begin + half], bias, labels, begin, lse, chips
        )
        scores.append(part)
        found += tail[0, :1]

    count = ndp * nmp * local
    message = jnp.concatenate([lse.reshape(-1), found])
    message = lax.all_to_all(jnp.broadcast_to(message[None], (ndp * nmp,) + message.shape), everyone, 0, 0)
    lse = jax.nn.logsumexp(message[:, :count], axis=0).reshape(chips, 1, -1)
    valid = labels >= 0
    loss = (jnp.sum(jnp.where(valid, lse, 0.0)) - jnp.sum(message[:, count])) / jnp.sum(valid.astype(F32))

    grad = table_grad(where, scores, lse, labels, near, far, fw)
    if not aligned:
        grad = grad.reshape(entries + 8, ndp, fw).transpose(1, 0, 2)
    grad = lax.all_to_all(grad.astype(F16), "dp", 0, 0)
    grad = grad[:, :entries].astype(F32) * jnp.exp2(-grad[:, entries : entries + 1].astype(F32))
    return (loss, grad.reshape(shard, fw))


def solution(mesh):
    in_specs = (
        P(("dp", "mp"), None, None),
        P(("dp", "mp"), None),
        P(("dp", "mp"), None),
        P(("dp", "mp")),
        P(),
        P(),
        P(),
        P(),
        P("mp", "dp"),
        P("mp"),
    )
    out_specs = (P(), P("mp", "dp"))

    return jax.shard_map(on_device, mesh=mesh, in_specs=in_specs, out_specs=out_specs, check_vma=False)
```

time: 378 us -> 174 us (0.46)
  waiting for transfers between devices: 238 us -> 67.7 us
  blocking collectives: 66.3 us -> 13 us
  matrix products: 41.5 us -> 2 us
  Pallas kernels: 0 us -> 31.1 us
  starting transfers between devices: 0.08 us -> 23.9 us
  between operations: 18 us -> 5.35 us
  local copies, waits for them, and re-layouts: 3.94 us -> 13.7 us
  other arithmetic: 9.25 us -> 16.1 us
    reduce_scatter x1 -> x0, waiting for transfers between devices: 188 us -> none  [on_device(): lax.psum_scatter(partial_grad, 'dp', scatter_dimension=1, tiled=True)]
    all_gather x1 -> x0, waiting for transfers between devices: 49.4 us -> none  [on_device(): lax.all_gather(embedding, 'dp', axis=1, tiled=True)]
    dot_general x3 -> x1, matrix products: 41.5 us -> 2 us  [transform(): pre = jnp.dot(rows, dense_weight, preferred_element_type=F32) + dense_bias]
    ppermute x0 -> x14, waiting for transfers between devices: none -> 39.4 us  [swap(): return lax.ppermute(x, axis, [(a, a ^ k) for a in range(n)])]
    pallas_call x0 -> x3, Pallas kernels: none -> 31.1 us  [the longest x2 18.6 us: score_rows(): pl.pallas_call(body, in_specs=[SCALAR] + [ANY] * (split + 2 * here) + [WH...]
    unnamed x2 -> x0, blocking collectives: 28.9 us -> none
    all_to_all x0 -> x2, waiting for transfers between devices: none -> 28.3 us  [the longest x1 23.4 us: on_device(): grad = lax.all_to_all(grad.astype(F16), 'dp', 0, 0)]
    all_gather x2 -> x0, blocking collectives: 24.9 us -> none  [the longest x1 15.8 us: on_device(): gathered = lax.all_gather(own_rows, 'mp', axis=0, tiled=True)]
  transfers between devices with their start and end apart: 2 -> 16, of which waited for: 2 -> 6; matrix products, arithmetic and copies ran while one was open for 3% -> 9% of each run, Pallas kernels for 0% -> 5%
where the time goes in v1:
time: 174 us; the launch traced here: 173 us
  waiting for transfers between devices  67.7 us (39%)
  Pallas kernels  31.1 us (18%)
  starting transfers between devices  23.9 us (14%)
  other arithmetic  16.1 us (9%)
  local copies, waits for them, and re-layouts  13.7 us (8%)
  blocking collectives  13 us (7%)
  between operations  5.35 us (3%)
  matrix products  2 us (1%)
    ppermute x14, waiting for transfers between devices, swap(): return lax.ppermute(x, axis, [(a, a ^ k) for a in range(n)])  39.4 us
    all_to_all x1, waiting for transfers between devices, on_device(): grad = lax.all_to_all(grad.astype(F16), 'dp', 0, 0)  23.4 us
    pallas_call x2, Pallas kernels, score_rows(): pl.pallas_call(body, in_specs=[SCALAR] + [ANY] * (split + 2 * here) + [WH...  18.6 us
    ppermute x14, starting transfers between devices, swap(): return lax.ppermute(x, axis, [(a, a ^ k) for a in range(n)])  14.7 us
    all_to_all x1, blocking collectives, on_device(): lax.all_to_all(jnp.broadcast_to(message[None], (ndp * nmp,) + message.sha...  13 us
    pallas_call x1, Pallas kernels, table_grad(): pl.pallas_call(body, in_specs=[SCALAR, WHOLE, WHOLE] + [ANY] * (held + 2...  12.6 us
    all_to_all x1, waiting for transfers between devices, on_device(): labels = lax.all_to_all(labels, everyone, 0, 0, tiled=True)  4.86 us
    all_to_all x1, starting transfers between devices, on_device(): labels = lax.all_to_all(labels, everyone, 0, 0, tiled=True)  4.86 us
  transfers between devices with their start and end apart: 16, of which 6 were waited for; matrix products, arithmetic and copies ran while one was open for 9% of the time, Pallas kernels for 5%

profile of v1, /device:TPU:0, one launch (start us, length us, event | category | flops | bytes accessed | tf_op | source)
XLA Modules:
  0.0 172.9 jit_solution(1740249952189970969)
XLA Ops:
  0.6 0.0 copy-start
  0.6 0.8 fusion.20
  1.5 0.7 compare_and_fusion
  2.1 2.2 %gather_fusion = bf16[80,1024]{1,0:T(8,128)(2,1)S(1)} fusion(bf16[512,1024]{1,0:T(8,128)(2,1)} %bitcast.60, s32[1024]{0:T(1024)S(1)} %pad_clamp_fusion), kind=kCustom, calls=%fused_computation | custom fusion | bytes 328000 | tf_op jit(solution)/shard_map/jit(take_along_axis)/gather | solution.py:243
  4.4 0.0 copy-start.3
  4.4 0.0 copy-start.4
  4.4 2.0 %fusion.22 = (f32[80]{0:T(128)S(1)}, f32[80,1024]{1,0:T(8,128)S(1)}) fusion(f32[1024]{0:T(1024)} %param.15, bf16[1024,1024]{1,0:T(8,128)(2,1)S(1)} %copy-done, bf16[80,1024]{1,0:T(8,128)(2,1)S(1)} %gather_fusion, pred[80]{0:T(512)(128)(4,1)S(1)} %compare_and_fusion), kind=kOutput, calls=%fused_computation.69 | convolution fusion | flops 173260720 | bytes 2593168 | tf_op jit(solution)/shard_map/dot_general | solution.py:23
  6.4 0.2 multiply_reduce_fusion
  6.6 0.1 broadcast_in_dim.63
  6.7 0.8 bitcast_dynamic-update-slice_fusion.3
  7.5 3.1 %collective-permute-start.4 = (bf16[80,1024]{1,0:T(8,128)(2,1)}, bf16[80,1024]{1,0:T(8,128)(2,1)}, u32[]{:S(2)}, u32[]{:S(2)}) collective-permute-start(bf16[80,1024]{1,0:T(8,128)(2,1)} %get-tuple-element.17), channel_id=1, source_target_pairs={{0,1},{1,0},{2,3},{3,2},{4,5},{5,4},{6,7},{7,6},{8,9},{9,8},{10,11... | collective-permute-start | bytes 491528 | tf_op jit(solution)/shard_map/ppermute | solution.py:19
  10.6 2.6 %collective-permute-start.5 = (bf16[80,1024]{1,0:T(8,128)(2,1)}, bf16[80,1024]{1,0:T(8,128)(2,1)}, u32[]{:S(2)}, u32[]{:S(2)}) collective-permute-start(bf16[80,1024]{1,0:T(8,128)(2,1)} %get-tuple-element.17), channel_id=1, source_target_pairs={{0,2},{1,3},{2,0},{3,1},{4,6},{5,7},{6,4},{7,5},{8,10},{9,11},{10,... | collective-permute-start | bytes 491528 | tf_op jit(solution)/shard_map/ppermute | solution.py:19
  13.2 2.7 %dynamic-slice_bitcast_fusion = (bf16[2,1024,128]{2,1,0:T(8,128)(2,1)S(1)}, bf16[2,1024,128]{2,1,0:T(8,128)(2,1)}, bf16[2,1024,128]{2,1,0:T(8,128)(2,1)}, bf16[2,1024,128]{2,1,0:T(8,128)(2,1)}) fusion(bf16[4,2,1024,128]{3,2,1,0:T(8,128)(2,1)} %bitcast.52, s32[]{:T(128)S(6)} %select_n.120, s32[]{:T(128)S(6)} %select_n.119, s32[]{:T(128)S(6)} %select_n.118, ...), kind=kLoop, calls=%fused_computation.4 | loop fusion | bytes 4194320 | tf_op jit(solution)/shard_map/jit(dynamic_index_in_dim)/squeeze | solution.py:229
  15.8 1.7 collective-permute-start
  17.5 1.5 collective-permute-start.1
  19.1 1.0 dynamic-slice_bitcast_fusion.4
  20.0 0.3 collective-permute-start.2
  20.4 0.9 bitcast_dynamic-update-slice_fusion.2
  21.3 0.0 copy-start.5
  21.3 4.6 %collective-permute-done.5 = bf16[80,1024]{1,0:T(8,128)(2,1)} collective-permute-done((bf16[80,1024]{1,0:T(8,128)(2,1)}, bf16[80,1024]{1,0:T(8,128)(2,1)}, u32[]{:S(2)}, u32[]{:S(2)}) %collective-permute-start.5) | collective-permute-done | bytes 163872 | tf_op jit(solution)/shard_map/ppermute | solution.py:19
  25.9 0.9 bitcast_dynamic-update-slice_fusion.1
  26.9 1.6 collective-permute-start.11
  28.4 1.5 collective-permute-start.7
  29.9 13.4 %collective-permute-done.2.refs_3_ = bf16[2,1024,128]{2,1,0:T(8,128)(2,1)S(1)} collective-permute-done((bf16[2,1024,128]{2,1,0:T(8,128)(2,1)S(1)}, bf16[2,1024,128]{2,1,0:T(8,128)(2,1)S(1)}, u32[]{:S(2)}, u32[]{:S(2)}) %collective-permute-start.2) | collective-permute-done | bytes 524320 | tf_op jit(solution)/shard_map/ppermute | solution.py:19
  43.3 1.4 collective-permute-start.8
  44.8 0.0 collective-permute-done.1.refs_2_
  44.8 1.0 constant_dynamic-slice_fusion.1
  45.8 0.0 collective-permute-done.refs_1_
  45.8 1.0 constant_dynamic-slice_fusion.2
  46.7 1.1 pad_maximum_fusion
  47.8 0.0 collective-permute-start.3
  47.9 0.5 collective-permute-start.12
  48.4 7.9 %collective-permute-done.11.refs_6_.refs_3_ = bf16[320,1024]{1,0:T(8,128)(2,1)} collective-permute-done((bf16[320,1024]{1,0:T(8,128)(2,1)S(1)}, bf16[320,1024]{1,0:T(8,128)(2,1)}, u32[]{:S(2)}, u32[]{:S(2)}) %collective-permute-start.11) | collective-permute-done | bytes 655392 | tf_op jit(solution)/shard_map/ppermute | solution.py:19
  56.3 0.0 collective-permute-start.13
  56.3 13.5 %collective-permute-done.7.refs_5_.refs_4_ = bf16[320,1024]{1,0:T(8,128)(2,1)} collective-permute-done((bf16[320,1024]{1,0:T(8,128)(2,1)S(1)}, bf16[320,1024]{1,0:T(8,128)(2,1)}, u32[]{:S(2)}, u32[]{:S(2)}) %collective-permute-start.7) | collective-permute-done | bytes 655392 | tf_op jit(solution)/shard_map/ppermute | solution.py:19
  69.8 0.5 collective-permute-start.10
  71.0 0.6 broadcast_in_dim.62
  71.6 4.9 %all-to-all-start = ((s32[32,1,80]{2,1,0:T(1,128)}), s32[32,1,80]{2,1,0:T(1,128)S(1)}, u32[]{:S(2)}, u32[]{:S(2)}) async-start(s32[32,1,80]{2,1,0:T(1,128)} %broadcast_in_dim.62), calls=%async_computation | async-start | bytes 32768 | tf_op jit(solution)/shard_map/all_to_all | solution.py:258
  76.5 0.6 pad_add_fusion.where_ref
  77.1 0.7 dynamic_slice.40
  77.8 1.0 copy.36.refs_9_.refs_11_
  78.8 4.9 %all-to-all-done = s32[32,1,80]{2,1,0:T(1,128)S(1)} async-done(((s32[32,1,80]{2,1,0:T(1,128)}), s32[32,1,80]{2,1,0:T(1,128)S(1)}, u32[]{:S(2)}, u32[]{:S(2)}) %all-to-all-start) | async-done | bytes 10272 | tf_op jit(solution)/shard_map/all_to_all | solution.py:258
  83.6 0.5 broadcast.124
  84.2 0.7 reduce.7
  84.9 0.7 reshape.199.refs_10_.labels_ref
  85.5 0.0 collective-permute-done.12.refs_7_.refs_6_
  85.6 9.3 %scores.2 = (f32[1,1024,1280]{2,1,0:T(8,128)}, f32[2,1,640]{2,1,0:T(1,128)}, f32[1,128]{1,0:T(1,128)}) custom-call(s32[3]{0:T(128)} %pad_add_fusion.where_ref, bf16[2,1024,128]{2,1,0:T(8,128)(2,1)} %get-tuple-element.21.refs_0_, bf16[2,1024,128]{2,1,0:T(8,128)(2,1)} %collective-permute-done.refs_1_, bf16[2,1024,128]{2,1,0:T(8,128)(2,1)} %collective-permute-done.1.refs_2_, ...), custom_call_target="tpu_custom_call" | custom-call | flops 2684354560 | bytes 5767168 | tf_op jit(solution)/shard_map/scores/pallas_call | solution.py:126
  94.9 0.0 copy-start.6
  94.9 9.2 %scores.3 = (f32[1,1024,1280]{2,1,0:T(8,128)}, f32[4,1,640]{2,1,0:T(1,128)}, f32[1,128]{1,0:T(1,128)}) custom-call(s32[3]{0:T(128)} %pad_add_fusion.where_ref, bf16[2,1024,128]{2,1,0:T(8,128)(2,1)} %get-tuple-element.21.refs_0_, bf16[2,1024,128]{2,1,0:T(8,128)(2,1)} %collective-permute-done.refs_1_, bf16[2,1024,128]{2,1,0:T(8,128)(2,1)} %collective-permute-done.1.refs_2_, ...), custom_call_target="tpu_custom_call" | custom-call | flops 2684354560 | bytes 5767168 | tf_op jit(solution)/shard_map/scores/pallas_call | solution.py:126
  104.2 0.7 reduce.4
  105.6 0.2 broadcast_in_dim.72
  105.8 13.0 %all_to_all.20 = f32[32,1,2561]{2,1,0:T(1,128)S(1)} all-to-all(f32[32,1,2561]{2,1,0:T(1,128)S(1)} %broadcast_in_dim.72), channel_id=1, replica_groups=mesh['dp'=8,'mp'=4] {'dp','mp'}, dimensions={0} | all-to-all | bytes 655616 | tf_op jit(solution)/shard_map/all_to_all | solution.py:270
  118.8 0.1 exponential_reduce_fusion
  119.0 0.6 fusion.15.lse_ref
  119.6 12.6 %table_grad.1 = f32[8,1032,128]{2,1,0:T(8,128)} custom-call(s32[3]{0:T(128)} %pad_add_fusion.where_ref, f32[4,1,640]{2,1,0:T(1,128)} %fusion.15.lse_ref, s32[4,1,640]{2,1,0:T(1,128)} %reshape.199.refs_10_.labels_ref, f32[1,1024,1280]{2,1,0:T(8,128)} %get-tuple-element.12.refs_0_, f32[1,1024,1280]{2,1,0:T(8,128)} %get-tuple-element.13.refs_1_, ...), custom_call_target="tpu_custom_call" | custom-call | flops 5368709120 | bytes 15728640 | tf_op jit(solution)/shard_map/table_grad/pallas_call | solution.py:196
  132.2 3.8 %convert_element_type.20 = f16[8,1032,128]{2,1,0:T(8,128)(2,1)} convert(f32[8,1032,128]{2,1,0:T(8,128)} %table_grad.1) | non-fusion elementwise | flops 1056768 | bytes 6340608 | tf_op jit(solution)/shard_map/convert_element_type | solution.py:278
  136.0 4.3 %all-to-all-start.2 = ((f16[8,1032,128]{2,1,0:T(8,128)(2,1)}), f16[8,1032,128]{2,1,0:T(8,128)(2,1)}, u32[]{:S(2)}, u32[]{:S(2)}) async-start(f16[8,1032,128]{2,1,0:T(8,128)(2,1)} %convert_element_type.20), calls=%async_computation.2 | async-start | bytes 4227072 | tf_op jit(solution)/shard_map/all_to_all | solution.py:278
  140.3 0.1 log.20
  140.4 0.1 reduce_max.14
  140.5 0.7 slice_reduce_fusion.1
  141.1 0.6 convert_reduce_fusion
  143.7 23.4 %all-to-all-done.2 = f16[8,1032,128]{2,1,0:T(8,128)(2,1)} async-done(((f16[8,1032,128]{2,1,0:T(8,128)(2,1)}), f16[8,1032,128]{2,1,0:T(8,128)(2,1)}, u32[]{:S(2)}, u32[]{:S(2)}) %all-to-all-start.2) | async-done | bytes 2113568 | tf_op jit(solution)/shard_map/all_to_all | solution.py:278
  167.1 0.7 fusion.18
  167.8 3.9 %convert_multiply_fusion = f32[8,1024,128]{2,1,0:T(8,128)} fusion(f16[8,1032,128]{2,1,0:T(8,128)(2,1)} %all-to-all-done.2, f32[8,128]{1,0:T(8,128)S(1)} %bitcast.63), kind=kLoop, calls=%fused_computation.1 | loop fusion | flops 2097152 | bytes 6295552 | tf_op jit(solution)/shard_map/mul | solution.py:279
  (32 shorter events, 0.2 us)
Async XLA Ops:
  0.6 3.7 %copy-start = (bf16[1024,1024]{1,0:T(8,128)(2,1)S(1)}, bf16[1024,1024]{1,0:T(8,128)(2,1)}, u32[]{:S(2)}) copy-start(bf16[1024,1024]{1,0:T(8,128)(2,1)} %param.14) | copy-start | bytes 6291460
  4.4 2.3 %copy-start.3 = (f32[1024]{0:T(1024)S(1)}, f32[1024]{0:T(1024)}, u32[]{:S(2)}) copy-start(f32[1024]{0:T(1024)} %param.17) | copy-start | bytes 12292
  4.4 2.3 %copy-start.4 = (f32[1024]{0:T(1024)S(1)}, f32[1024]{0:T(1024)}, u32[]{:S(2)}) copy-start(f32[1024]{0:T(1024)} %param.16) | copy-start | bytes 12292
  7.5 12.5 %collective-permute-start.4 = (bf16[80,1024]{1,0:T(8,128)(2,1)}, bf16[80,1024]{1,0:T(8,128)(2,1)}, u32[]{:S(2)}, u32[]{:S(2)}) collective-permute-start(bf16[80,1024]{1,0:T(8,128)(2,1)} %get-tuple-element.17), channel_id=1, source_target_pairs={{0,1},{1,0},{2,3},{3,2},{4,5},{5,4},{6,7},{7,6},{8,9},{9,8},{10,11... | collective-permute-start | bytes 491528 | tf_op jit(solution)/shard_map/ppermute | solution.py:19
  10.6 15.3 %collective-permute-start.5 = (bf16[80,1024]{1,0:T(8,128)(2,1)}, bf16[80,1024]{1,0:T(8,128)(2,1)}, u32[]{:S(2)}, u32[]{:S(2)}) collective-permute-start(bf16[80,1024]{1,0:T(8,128)(2,1)} %get-tuple-element.17), channel_id=1, source_target_pairs={{0,2},{1,3},{2,0},{3,1},{4,6},{5,7},{6,4},{7,5},{8,10},{9,11},{10,... | collective-permute-start | bytes 491528 | tf_op jit(solution)/shard_map/ppermute | solution.py:19
  13.2 13.7 %collective-permute-start.6 = (bf16[80,1024]{1,0:T(8,128)(2,1)}, bf16[80,1024]{1,0:T(8,128)(2,1)S(1)}, u32[]{:S(2)}, u32[]{:S(2)}) collective-permute-start(bf16[80,1024]{1,0:T(8,128)(2,1)} %get-tuple-element.17), channel_id=1, source_target_pairs={{0,3},{1,2},{2,1},{3,0},{4,7},{5,6},{6,5},{7,4},{8,11},{9,10},{10,... | collective-permute-start | bytes 491528 | tf_op jit(solution)/shard_map/ppermute | solution.py:19
  15.8 29.9 %collective-permute-start = (bf16[2,1024,128]{2,1,0:T(8,128)(2,1)}, bf16[2,1024,128]{2,1,0:T(8,128)(2,1)}, u32[]{:S(2)}, u32[]{:S(2)}) collective-permute-start(bf16[2,1024,128]{2,1,0:T(8,128)(2,1)} %get-tuple-element.20), channel_id=1, source_target_pairs={{0,8},{4,12},{8,0},{12,4},{16,24},{20,28},{24,16},{28,20},{1,9},{5... | collective-permute-start | bytes 1572872 | tf_op jit(solution)/shard_map/ppermute | solution.py:19
  17.5 27.2 %collective-permute-start.1 = (bf16[2,1024,128]{2,1,0:T(8,128)(2,1)}, bf16[2,1024,128]{2,1,0:T(8,128)(2,1)}, u32[]{:S(2)}, u32[]{:S(2)}) collective-permute-start(bf16[2,1024,128]{2,1,0:T(8,128)(2,1)} %get-tuple-element.19), channel_id=1, source_target_pairs={{0,16},{4,20},{8,24},{12,28},{16,0},{20,4},{24,8},{28,12},{1,17},{... | collective-permute-start | bytes 1572872 | tf_op jit(solution)/shard_map/ppermute | solution.py:19
  20.0 23.3 %collective-permute-start.2 = (bf16[2,1024,128]{2,1,0:T(8,128)(2,1)S(1)}, bf16[2,1024,128]{2,1,0:T(8,128)(2,1)S(1)}, u32[]{:S(2)}, u32[]{:S(2)}) collective-permute-start(bf16[2,1024,128]{2,1,0:T(8,128)(2,1)S(1)} %get-tuple-element.18), channel_id=1, source_target_pairs={{0,24},{4,28},{8,16},{12,20},{16,8},{20,12},{24,0},{28,4},{1,25},{... | collective-permute-start | bytes 1572872 | tf_op jit(solution)/shard_map/ppermute | solution.py:19
  21.3 49.7 %copy-start.5 = (s32[1,80]{1,0:T(1,128)S(1)}, s32[1,80]{1,0:T(1,128)}, u32[]{:S(2)}) copy-start(s32[1,80]{1,0:T(1,128)} %param.12) | copy-start | bytes 964
  26.8 51.9 %copy-start.1 = (bf16[4,80,1024]{2,1,0:T(8,128)(2,1)}, bf16[4,80,1024]{2,1,0:T(8,128)(2,1)S(1)}, u32[]{:S(2)}) copy-start(bf16[4,80,1024]{2,1,0:T(8,128)(2,1)S(1)} %bitcast_dynamic-update-slice_fusion) | copy-start | bytes 1966084
  26.9 29.4 %collective-permute-start.11 = (bf16[320,1024]{1,0:T(8,128)(2,1)S(1)}, bf16[320,1024]{1,0:T(8,128)(2,1)}, u32[]{:S(2)}, u32[]{:S(2)}) collective-permute-start(bf16[320,1024]{1,0:T(8,128)(2,1)S(1)} %bitcast.54), channel_id=1, source_target_pairs={{0,8},{4,12},{8,0},{12,4},{16,24},{20,28},{24,16},{28,20},{1,9},{5... | collective-permute-start | bytes 1966088 | tf_op jit(solution)/shard_map/ppermute | solution.py:19
  28.4 41.4 %collective-permute-start.7 = (bf16[320,1024]{1,0:T(8,128)(2,1)S(1)}, bf16[320,1024]{1,0:T(8,128)(2,1)}, u32[]{:S(2)}, u32[]{:S(2)}) collective-permute-start(bf16[320,1024]{1,0:T(8,128)(2,1)S(1)} %bitcast.55), channel_id=1, source_target_pairs={{0,16},{4,20},{8,24},{12,28},{16,0},{20,4},{24,8},{28,12},{1,17},{... | collective-permute-start | bytes 1966088 | tf_op jit(solution)/shard_map/ppermute | solution.py:19
  43.3 2.4 %copy-start.2 = (bf16[2,1024,128]{2,1,0:T(8,128)(2,1)}, bf16[2,1024,128]{2,1,0:T(8,128)(2,1)S(1)}, u32[]{:S(2)}) copy-start(bf16[2,1024,128]{2,1,0:T(8,128)(2,1)S(1)} %collective-permute-done.2.refs_3_) | copy-start | bytes 1572868
  43.3 26.5 %collective-permute-start.8 = (bf16[320,1024]{1,0:T(8,128)(2,1)S(1)}, bf16[320,1024]{1,0:T(8,128)(2,1)}, u32[]{:S(2)}, u32[]{:S(2)}) collective-permute-start(bf16[320,1024]{1,0:T(8,128)(2,1)S(1)} %bitcast.56), channel_id=1, source_target_pairs={{0,24},{4,28},{8,16},{12,20},{16,8},{20,12},{24,0},{28,4},{1,25},{... | collective-permute-start | bytes 1966088 | tf_op jit(solution)/shard_map/ppermute | solution.py:19
  47.8 37.7 %collective-permute-start.3 = (bf16[4,1024,128]{2,1,0:T(8,128)(2,1)}, bf16[4,1024,128]{2,1,0:T(8,128)(2,1)}, u32[]{:S(2)}, u32[]{:S(2)}) collective-permute-start(bf16[4,1024,128]{2,1,0:T(8,128)(2,1)} %pad_maximum_fusion), channel_id=1, source_target_pairs={{0,4},{4,0},{8,12},{12,8},{16,20},{20,16},{24,28},{28,24},{1,5},{5... | collective-permute-start | bytes 3145736 | tf_op jit(solution)/shard_map/ppermute | solution.py:19
  47.9 37.7 %collective-permute-start.12 = (bf16[320,1024]{1,0:T(8,128)(2,1)S(1)}, bf16[320,1024]{1,0:T(8,128)(2,1)}, u32[]{:S(2)}, u32[]{:S(2)}) collective-permute-start(bf16[320,1024]{1,0:T(8,128)(2,1)S(1)} %bitcast.57), channel_id=1, source_target_pairs={{0,4},{4,0},{8,12},{12,8},{16,20},{20,16},{24,28},{28,24},{1,5},{5... | collective-permute-start | bytes 1966088 | tf_op jit(solution)/shard_map/ppermute | solution.py:19
  56.3 29.3 %collective-permute-start.13 = (bf16[320,1024]{1,0:T(8,128)(2,1)}, bf16[320,1024]{1,0:T(8,128)(2,1)}, u32[]{:S(2)}, u32[]{:S(2)}) collective-permute-start(bf16[320,1024]{1,0:T(8,128)(2,1)} %collective-permute-done.11.refs_6_.refs_3_), channel_id=1, source_target_pairs={{0,4},{4,0},{8,12},{12,8},{16,20},{20,16},{24,28},{28,24},{1,5},{5... | collective-permute-start | bytes 1966088 | tf_op jit(solution)/shard_map/ppermute | solution.py:19
  69.8 25.1 %collective-permute-start.9 = (bf16[320,1024]{1,0:T(8,128)(2,1)}, bf16[320,1024]{1,0:T(8,128)(2,1)}, u32[]{:S(2)}, u32[]{:S(2)}) collective-permute-start(bf16[320,1024]{1,0:T(8,128)(2,1)} %collective-permute-done.7.refs_5_.refs_4_), channel_id=1, source_target_pairs={{0,4},{4,0},{8,12},{12,8},{16,20},{20,16},{24,28},{28,24},{1,5},{5... | collective-permute-start | bytes 1966088 | tf_op jit(solution)/shard_map/ppermute | solution.py:19
  69.8 25.1 %collective-permute-start.10 = (bf16[320,1024]{1,0:T(8,128)(2,1)}, bf16[320,1024]{1,0:T(8,128)(2,1)}, u32[]{:S(2)}, u32[]{:S(2)}) collective-permute-start(bf16[320,1024]{1,0:T(8,128)(2,1)} %collective-permute-done.8.refs_6_.refs_5_), channel_id=1, source_target_pairs={{0,4},{4,0},{8,12},{12,8},{16,20},{20,16},{24,28},{28,24},{1,5},{5... | collective-permute-start | bytes 1966088 | tf_op jit(solution)/shard_map/ppermute | solution.py:19
  71.6 12.1 %all-to-all-start = ((s32[32,1,80]{2,1,0:T(1,128)}), s32[32,1,80]{2,1,0:T(1,128)S(1)}, u32[]{:S(2)}, u32[]{:S(2)}) async-start(s32[32,1,80]{2,1,0:T(1,128)} %broadcast_in_dim.62), calls=%async_computation | async-start | bytes 32768 | tf_op jit(solution)/shard_map/all_to_all | solution.py:258
  94.9 10.0 %copy-start.6 = (f32[1,128]{1,0:T(1,128)S(1)}, f32[1,128]{1,0:T(1,128)}, u32[]{:S(2)}) copy-start(f32[1,128]{1,0:T(1,128)} %get-tuple-element.10) | copy-start | bytes 1540
  136.0 31.2 %all-to-all-start.2 = ((f16[8,1032,128]{2,1,0:T(8,128)(2,1)}), f16[8,1032,128]{2,1,0:T(8,128)(2,1)}, u32[]{:S(2)}, u32[]{:S(2)}) async-start(f16[8,1032,128]{2,1,0:T(8,128)(2,1)} %convert_element_type.20), calls=%async_computation.2 | async-start | bytes 4227072 | tf_op jit(solution)/shard_map/all_to_all | solution.py:278
